TPU v7x, 512 devices: a whole 4x4x16 slice. The times are simulated.
512 devices in a mesh: row: 32 (over y_hi, z), col: 16 (over x, y_lo, core).
Axes of the slice: x: 4, y: 4 (y_hi: 2, y_lo: 2; y = y_hi * 2 + y_lo), z: 16, core: 2. Of those that a mesh axis runs over, the one named last changes fastest.
Arguments:
- incoming_evolution_embedding: bfloat16 [64, 512, 64], P(None, 'row'), may hold values from -6 to 6
- learned_affine_stretch: float32 [64], replicated, may hold values from 0.5 to 1.5
- learned_affine_offset: float32 [64], replicated, may hold values from -3 to 3
- lefthand_mapping_tensor: bfloat16 [64, 32], replicated, may hold values from -0.75 to 0.75
- righthand_mapping_tensor: bfloat16 [64, 32], replicated, may hold values from -0.75 to 0.75
- final_outer_matrix: bfloat16 [1024, 128], replicated, may hold values from -0.1875 to 0.1875
- residue_couple_cotangent: bfloat16 [512, 512, 128], P('row', 'col'), may hold values from -6 to 6
Outputs:
- alignment_gradient: bfloat16 [64, 512, 64], P('col', 'row')
- left_weight_gradient: float32 [64, 32], replicated
- right_weight_gradient: float32 [64, 32], replicated
- output_weight_gradient: float32 [1024, 128], replicated
All inputs are finite; a program needn't handle non-finite values.
Results may differ from a plain program's by a relative error of at most 0.0064.
Values may be sent and summed in bfloat16 or wider, within the bound.
No kernel may reach another device: no remote copies, remote signals or barrier semaphores. Data moves between devices by JAX's collectives and lax.ppermute only.
A program may use at most 64 MiB of HBM per device.

v0:
```python
import math
import jax
import jax.numpy as jnp
from jax import lax
from jax.sharding import PartitionSpec as P

highest = lax.Precision.HIGHEST


def broadcast(x, axis, root):
    mine = lax.axis_index(axis) == root
    return lax.psum(jnp.where(mine, x, jnp.zeros_like(x)), axis)


def standardize_features(values, learned_affine_stretch, learned_affine_offset):
    values = values.astype(jnp.float32)
    mean_value = jnp.mean(values, -1, keepdims=True)
    centred = values - mean_value
    variance = jnp.mean(centred * centred, -1, keepdims=True)
    reciprocal_spread_std = lax.rsqrt(variance + 1e-05)
    multiplied_activations = centred * reciprocal_spread_std
    standardized_activations = (
        multiplied_activations * learned_affine_stretch + learned_affine_offset
    ).astype(jnp.bfloat16)
    return (multiplied_activations, reciprocal_spread_std, standardized_activations)


def project(standardized_activations, weight):
    array_shape = standardized_activations.shape
    flat = jnp.dot(
        standardized_activations.reshape(-1, array_shape[-1]),
        weight,
        preferred_element_type=jnp.float32,
    )
    return flat.astype(jnp.bfloat16).reshape(array_shape[:-1] + (weight.shape[1],))


def outer_block(left_block, right_matrix, grad_block, final_outer_matrix, element_number, hidden):
    rows = grad_block.shape[0]
    cols = grad_block.shape[1]
    outer = lax.dot_general(
        left_block, right_matrix, (((0,), (0,)), ((), ())), preferred_element_type=jnp.float32
    )
    outer = (outer * (1.0 / element_number)).astype(jnp.bfloat16)
    outer = (
        outer.reshape(rows, hidden, cols, hidden)
        .transpose(0, 2, 1, 3)
        .reshape(rows * cols, hidden * hidden)
    )
    flat_grad = grad_block.reshape(rows * cols, grad_block.shape[2])
    weight_term = lax.dot_general(
        outer, flat_grad, (((0,), (0,)), ((), ())), preferred_element_type=jnp.float32
    )
    outer_grad = lax.dot_general(
        flat_grad, final_outer_matrix, (((1,), (1,)), ((), ())), preferred_element_type=jnp.float32
    )
    outer_grad = outer_grad.astype(jnp.bfloat16)
    outer_grad = (
        outer_grad.reshape(rows, cols, hidden, hidden)
        .transpose(0, 2, 1, 3)
        .reshape(rows * hidden, cols * hidden)
    )
    left_term = lax.dot_general(
        outer_grad, right_matrix, (((1,), (1,)), ((), ())), preferred_element_type=jnp.float32
    )
    left_term = (
        (left_term * (1.0 / element_number))
        .reshape(rows, hidden, element_number)
        .transpose(2, 0, 1)
    )
    right_term = jnp.dot(left_block, outer_grad, preferred_element_type=jnp.float32) * (
        1.0 / element_number
    )
    return (weight_term, left_term, right_term)


def norm_gradient_pass(
    left_gradient,
    right_gradient,
    lefthand_mapping_tensor,
    righthand_mapping_tensor,
    multiplied_activations,
    reciprocal_spread_std,
    learned_affine_stretch,
):
    hidden = lefthand_mapping_tensor.shape[1]
    hidden_grad = jnp.dot(
        left_gradient.reshape(-1, hidden),
        lefthand_mapping_tensor.astype(jnp.float32).T,
        precision=highest,
    )
    hidden_grad = hidden_grad + jnp.dot(
        right_gradient.reshape(-1, hidden),
        righthand_mapping_tensor.astype(jnp.float32).T,
        precision=highest,
    )
    hidden_grad = hidden_grad.reshape(multiplied_activations.shape) * learned_affine_stretch
    mean_one = jnp.mean(hidden_grad, -1, keepdims=True)
    mean_two = jnp.mean(hidden_grad * multiplied_activations, -1, keepdims=True)
    return (
        reciprocal_spread_std * (hidden_grad - mean_one - multiplied_activations * mean_two)
    ).astype(jnp.bfloat16)


def weight_grad(standardized_activations, factor_grad):
    feature_width = standardized_activations.shape[-1]
    hidden = factor_grad.shape[-1]
    return lax.dot_general(
        standardized_activations.astype(jnp.float32).reshape(-1, feature_width),
        factor_grad.reshape(-1, hidden),
        (((0,), (0,)), ((), ())),
        precision=highest,
        preferred_element_type=jnp.float32,
    )


def on_device(
    incoming_evolution_embedding,
    learned_affine_stretch,
    learned_affine_offset,
    lefthand_mapping_tensor,
    righthand_mapping_tensor,
    final_outer_matrix,
    residue_couple_cotangent,
):
    homolog_number, residue_slices, feature_width = incoming_evolution_embedding.shape
    hidden = lefthand_mapping_tensor.shape[1]
    cohort_extent = lax.axis_size("row") // lax.axis_size("col")
    residue_position = lax.axis_index("col")
    row_index = lax.axis_index("row")
    multiplied_activations, reciprocal_spread_std, standardized_activations = standardize_features(
        incoming_evolution_embedding, learned_affine_stretch, learned_affine_offset
    )
    left_factor = project(standardized_activations, lefthand_mapping_tensor)
    divide_pieces = []
    for cohort_rank in range(cohort_extent):
        divide_pieces.append(
            broadcast(
                incoming_evolution_embedding, "row", cohort_extent * residue_position + cohort_rank
            )
        )
    fetched = jnp.concatenate(divide_pieces, 1)
    fetched_normed = standardize_features(fetched, learned_affine_stretch, learned_affine_offset)[2]
    right_cols = project(fetched_normed, righthand_mapping_tensor)
    tok_cols = right_cols.shape[1]
    right_matrix = right_cols.reshape(homolog_number, tok_cols * hidden)
    block_rows = math.gcd(residue_slices, 8)
    weight_acc = jnp.zeros((hidden * hidden, final_outer_matrix.shape[1]), jnp.float32)
    right_acc = jnp.zeros((homolog_number, tok_cols * hidden), jnp.float32)
    left_parts = []
    for offset in range(0, residue_slices, block_rows):
        left_block = left_factor[:, offset : offset + block_rows, :].reshape(
            homolog_number, block_rows * hidden
        )
        grad_block = residue_couple_cotangent[offset : offset + block_rows]
        weight_term, left_term, right_term = outer_block(
            left_block, right_matrix, grad_block, final_outer_matrix, homolog_number, hidden
        )
        weight_acc = weight_acc + weight_term
        right_acc = right_acc + right_term
        left_parts.append(left_term)
    left_partial = jnp.concatenate(left_parts, 1)
    left_gradient = lax.psum_scatter(left_partial, "col", scatter_dimension=0, tiled=True)
    seq_share = homolog_number // lax.axis_size("col")
    seq_first = residue_position * seq_share
    right_partial = right_acc.reshape(homolog_number, tok_cols, hidden)
    right_total = lax.psum(right_partial, "row")
    own_part = lax.dynamic_slice_in_dim(
        right_total, row_index % cohort_extent * residue_slices, residue_slices, 1
    )
    right_rows = broadcast(own_part, "col", row_index // cohort_extent)
    right_gradient = lax.dynamic_slice_in_dim(right_rows, seq_first, seq_share, 0)
    scaled_own_part = lax.dynamic_slice_in_dim(multiplied_activations, seq_first, seq_share, 0)
    inverse_own_scale = lax.dynamic_slice_in_dim(reciprocal_spread_std, seq_first, seq_share, 0)
    normed_own = lax.dynamic_slice_in_dim(standardized_activations, seq_first, seq_share, 0)
    alignment_gradient = norm_gradient_pass(
        left_gradient,
        right_gradient,
        lefthand_mapping_tensor,
        righthand_mapping_tensor,
        scaled_own_part,
        inverse_own_scale,
        learned_affine_stretch,
    )
    left_weight = weight_grad(normed_own, left_gradient)
    right_weight = weight_grad(normed_own, right_gradient)
    out_total, left_total, right_sum = lax.psum(
        (weight_acc, left_weight, right_weight), ("row", "col")
    )
    tokens = residue_slices * lax.axis_size("row")
    return (
        alignment_gradient,
        left_total * (1.0 / tokens),
        right_sum * (1.0 / tokens),
        out_total * (1.0 / tokens),
    )


def solution(mesh):
    in_specs = (P(None, "row", None), P(), P(), P(), P(), P(), P("row", "col", None))
    out_specs = (P("col", "row", None), P(), P(), P())
    return jax.shard_map(
        on_device, mesh=mesh, in_specs=in_specs, out_specs=out_specs, check_vma=False
    )
```

profile of v0, /device:TPU:1, one launch (start us, length us, event | category | flops | bytes accessed | tf_op | source)
XLA Modules:
  0.0 1406.3 jit_solution(8164136535824600437)
XLA Ops:
  7.2 1.8 broadcast_select_fusion.1
  12.7 1.6 reshape.145
  14.2 2.1 copy.62
  16.4 3.6 reshape.146
  23.3 1.6 reshape.149
  24.8 2.1 copy.61
  27.0 3.6 reshape.150
  31.1 1.8 copy.51
  33.0 265.5 %all-reduce.13.cloned.1.call-done = (bf16[64,16,64]{2,1,0:T(8,128)(2,1)}, bf16[64,16,64]{2,1,0:T(8,128)(2,1)}) async-done(((bf16[64,16,64]{2,1,0:T(8,128)(2,1)}, bf16[64,16,64]{2,1,0:T(8,128)(2,1)}), (bf16[64,16,64]{2,1,0:T(8,128)(2,1)}, bf16[64,16,64]{2,1,0:T(8,128)(2,1)})) %all-reduce.13.cloned.1.call-update) | async-done | bytes 262160 | tf_op jit(solution)/shard_map/psum | solution.py:12
  299.7 1.4 fusion.10
  305.9 290.3 %all-reduce.7.cloned.1.call-done = f32[64,32,32]{2,1,0:T(8,128)} async-done(((f32[64,32,32]{2,1,0:T(8,128)}), f32[64,32,32]{2,1,0:T(8,128)}) %all-reduce.7.cloned.1.call-update) | async-done | bytes 262160 | tf_op jit(solution)/shard_map/psum | solution.py:167
  596.2 1.9 dynamic-slice_select_fusion
  598.3 2.9 reshape.160
  601.2 2.1 copy.60
  603.3 3.6 reshape.161
  608.0 2.8 reshape.162
  610.9 2.1 copy.59
  613.0 3.6 reshape.163
  619.8 129.4 %all-reduce.9.cloned.1.call-done = f32[64,16,32]{2,1,0:T(8,128)} async-done(((f32[64,16,32]{2,1,0:T(8,128)}), f32[64,16,32]{2,1,0:T(8,128)}) %all-reduce.9.cloned.1.call-update) | async-done | bytes 131088 | tf_op jit(solution)/shard_map/psum | solution.py:12
  750.9 470.0 %all-reduce.11.cloned.1.call-done = f32[1024,128]{1,0:T(8,128)} async-done(((f32[1024,128]{1,0:T(8,128)}), f32[1024,128]{1,0:T(8,128)}) %all-reduce.11.cloned.1.call-update) | async-done | bytes 524304 | tf_op jit(solution)/shard_map/psum | solution.py:187
  1220.9 1.9 broadcast_multiply_fusion
  1222.8 64.8 %reduce-scatter.2.cloned.1.call-done = f32[4,16,32]{2,1,0:T(8,128)} async-done(((f32[64,16,32]{2,1,0:T(8,128)}), f32[4,16,32]{2,1,0:T(8,128)}) %reduce-scatter.2.cloned.1.call-update) | async-done | bytes 8208 | tf_op jit(solution)/shard_map/reduce_scatter | solution.py:163
  1291.5 106.2 %all-reduce = (f32[64,32]{0,1:T(8,128)S(1)}, f32[64,32]{0,1:T(8,128)S(1)}) all-reduce(f32[64,32]{0,1:T(8,128)S(1)} %convolution_bitcast_fusion.1, f32[64,32]{0,1:T(8,128)S(1)} %convolution_bitcast_fusion), channel_id=1, replica_groups=mesh['row'=32,'col'=16] {'row','col'}, use_global_device_ids=true, to_apply=%region_11.12 | all-reduce | flops 4096 | bytes 32768 | tf_op jit(solution)/shard_map/psum | solution.py:187
  1398.3 1.5 multiply_convert_fusion
  (101 shorter events, 24.0 us)
Async XLA Ops:
  7.2 4.6 copy-start
  7.2 4.5 copy-start.14
  7.2 291.3 %all-reduce.13.cloned.1.call-start = ((), (), s32[]{:S(2)}) async-start(), calls=%async_computation.5 | async-start | bytes 1048576 | tf_op jit(solution)/shard_map/psum | solution.py:12
  9.1 587.1 %all-reduce.7.cloned.1.call-start = ((), (), s32[]{:S(2)}) async-start(), calls=%async_computation.2 | async-start | bytes 2097152 | tf_op jit(solution)/shard_map/psum | solution.py:167
  11.7 8.3 copy-start.13
  16.4 3.6 copy-start.1
  16.4 3.6 copy-start.17
  16.4 3.6 copy-start.20
  16.4 4.8 copy-start.15
  21.2 0.7 copy-start.5
  27.0 3.7 copy-start.6
  32.9 269.0 %copy-start.18 = (f32[64]{0:T(128)S(1)}, f32[64]{0:T(128)}, u32[]{:S(2)}) copy-start(f32[64]{0:T(128)} %param.8) | copy-start | bytes 772
  32.9 269.0 %copy-start.21 = (f32[64]{0:T(128)S(1)}, f32[64]{0:T(128)}, u32[]{:S(2)}) copy-start(f32[64]{0:T(128)} %param.9) | copy-start | bytes 772
  33.0 716.2 %all-reduce.9.cloned.1.call-start = ((), (), s32[]{:S(2)}) async-start(), calls=%async_computation.3 | async-start | bytes 1048576 | tf_op jit(solution)/shard_map/psum | solution.py:12
  298.5 2.6 copy-start.2
  298.5 2.6 copy-start.3
  298.5 4.1 copy-start.16
  301.1 2.5 copy-start.12
  598.1 622.8 %all-reduce.11.cloned.1.call-start = ((), (), s32[]{:S(2)}) async-start(), calls=%async_computation.4 | async-start | bytes 1048576 | tf_op jit(solution)/shard_map/psum | solution.py:187
  603.3 3.6 copy-start.10
  613.0 3.6 copy-start.4
  613.0 3.6 copy-start.8
  618.2 670.3 %copy-start.19 = (f32[64]{0:T(128)S(1)}, f32[64]{0:T(128)}, u32[]{:S(2)}) copy-start(f32[64]{0:T(128)} %param.8) | copy-start | bytes 772
  618.3 669.3 %reduce-scatter.2.cloned.1.call-start = ((), (), s32[]{:S(2)}) async-start(), calls=%async_computation.1 | async-start | bytes 557056 | tf_op jit(solution)/shard_map/reduce_scatter | solution.py:163
  (3 other events, 1.9 us)
Sparse Core Ops, SparseCore 0:
  11.5 286.9 all-reduce.12
  301.4 294.7 all-reduce.6
  599.7 149.4 all-reduce.8
  754.5 466.3 all-reduce.10
  1223.5 64.0 reduce-scatter.1
where the time goes:
time: 1410 us
  waiting for transfers between devices  1220 us (87%)
  blocking collectives  106 us (8%)
  local copies, waits for them, and re-layouts  38.3 us (3%)
  other arithmetic  16.7 us (1%)
  between operations  14.3 us (1%)
    psum x1, waiting for transfers between devices, on_device(): lax.psum((weight_acc, left_weight, right_weight), ('row', 'col'))  470 us
    psum x2, waiting for transfers between devices, broadcast(): return lax.psum(jnp.where(mine, x, jnp.zeros_like(x)), axis)  395 us
    psum x1, waiting for transfers between devices, on_device(): right_total = lax.psum(right_partial, 'row')  290 us
    psum x1, blocking collectives, on_device(): lax.psum((weight_acc, left_weight, right_weight), ('row', 'col'))  106 us
    reduce_scatter x1, waiting for transfers between devices, on_device(): lax.psum_scatter(left_partial, 'col', scatter_dimension=0, tiled=True)  64.8 us
  transfers between devices with their start and end apart: 5, of which 5 were waited for; matrix products, arithmetic and copies ran while one was open for 4% of the time, Pallas kernels for 0%

commit v1 on v0

--- a/solution.py
+++ b/solution.py
@@ -5,6 +5,11 @@
 from jax.sharding import PartitionSpec as P
 
 highest = lax.Precision.HIGHEST
+
+
+def one_after_other(value, axis_one, axis_two):
+    partial = lax.psum(value, axis_one)
+    return lax.psum(partial, axis_two)
 
 
 def broadcast(x, axis, root):
@@ -184,8 +189,8 @@
     )
     left_weight = weight_grad(normed_own, left_gradient)
     right_weight = weight_grad(normed_own, right_gradient)
-    out_total, left_total, right_sum = lax.psum(
-        (weight_acc, left_weight, right_weight), ("row", "col")
+    out_total, left_total, right_sum = one_after_other(
+        (weight_acc, left_weight, right_weight), "row", "col"
     )
     tokens = residue_slices * lax.axis_size("row")
     return (

time: 1410 us -> 1060 us (0.75)
  waiting for transfers between devices: 1220 us -> 780 us
  blocking collectives: 106 us -> 198 us
    psum x1 -> x0, waiting for transfers between devices: 470 us -> none  [on_device(): lax.psum((weight_acc, left_weight, right_weight), ('row', 'col'))]
    psum x1 -> x2, blocking collectives: 106 us -> 198 us  [the longest x1 121 us: one_after_other(): partial = lax.psum(value, axis_one)]
    reduce_scatter x1, waiting for transfers between devices: 64.8 us -> 83.3 us  [on_device(): lax.psum_scatter(left_partial, 'col', scatter_dimension=0, tiled=True)]
  transfers between devices with their start and end apart: 5 -> 4, of which waited for: 5 -> 4; matrix products, arithmetic and copies ran while one was open for 4% -> 3% of each run, Pallas kernels for 0% -> 0%
where the time goes in v1:
time: 1060 us
  waiting for transfers between devices  780 us (74%)
  blocking collectives  198 us (19%)
  local copies, waits for them, and re-layouts  39.4 us (4%)
  other arithmetic  17.7 us (2%)
  between operations  14.3 us (1%)
    psum x2, waiting for transfers between devices, broadcast(): return lax.psum(jnp.where(mine, x, jnp.zeros_like(x)), axis)  402 us
    psum x1, waiting for transfers between devices, on_device(): right_total = lax.psum(right_partial, 'row')  295 us
    psum x1, blocking collectives, one_after_other(): partial = lax.psum(value, axis_one)  121 us
    reduce_scatter x1, waiting for transfers between devices, on_device(): lax.psum_scatter(left_partial, 'col', scatter_dimension=0, tiled=True)  83.3 us
    psum x1, blocking collectives, one_after_other(): return lax.psum(partial, axis_two)  77 us
  transfers between devices with their start and end apart: 4, of which 4 were waited for; matrix products, arithmetic and copies ran while one was open for 3% of the time, Pallas kernels for 0%

profile of v1, /device:TPU:1, one launch (start us, length us, event | category | flops | bytes accessed | tf_op | source)
XLA Modules:
  0.0 1059.6 jit_solution(8546771391652429842)
XLA Ops:
  7.3 1.9 broadcast_select_fusion.1
  11.7 1.8 add_convert_fusion
  15.8 1.6 reshape.145
  17.4 2.1 copy.62
  19.6 3.6 reshape.146
  24.5 1.6 reshape.149
  26.1 2.1 copy.61
  28.3 3.6 reshape.150
  32.3 1.8 copy.51
  34.1 264.4 %all-reduce.13.cloned.1.call-done = (bf16[64,16,64]{2,1,0:T(8,128)(2,1)}, bf16[64,16,64]{2,1,0:T(8,128)(2,1)}) async-done(((bf16[64,16,64]{2,1,0:T(8,128)(2,1)}, bf16[64,16,64]{2,1,0:T(8,128)(2,1)}), (bf16[64,16,64]{2,1,0:T(8,128)(2,1)}, bf16[64,16,64]{2,1,0:T(8,128)(2,1)})) %all-reduce.13.cloned.1.call-update) | async-done | bytes 262160 | tf_op jit(solution)/shard_map/psum | solution.py:17
  299.9 1.7 multiply_reduce_fusion
  306.8 2.8 reshape.160
  309.7 2.1 copy.60
  311.8 3.6 reshape.161
  316.5 2.8 reshape.162
  319.4 2.1 copy.59
  321.6 3.6 reshape.163
  328.3 294.6 %all-reduce.9.cloned.1.call-done = (f32[64,32,32]{2,1,0:T(8,128)}, f32[1024,128]{1,0:T(8,128)}) async-done(((f32[64,32,32]{2,1,0:T(8,128)}, f32[1024,128]{1,0:T(8,128)}), (f32[64,32,32]{2,1,0:T(8,128)}, f32[1024,128]{1,0:T(8,128)})) %all-reduce.9.cloned.1.call-update) | async-done | bytes 786448 | tf_op jit(solution)/shard_map/psum | solution.py:172
  622.9 1.9 dynamic-slice_select_fusion
  625.5 83.3 %reduce-scatter.2.cloned.1.call-done = f32[4,16,32]{2,1,0:T(8,128)} async-done(((f32[64,16,32]{2,1,0:T(8,128)}), f32[4,16,32]{2,1,0:T(8,128)}) %reduce-scatter.2.cloned.1.call-update) | async-done | bytes 8208 | tf_op jit(solution)/shard_map/reduce_scatter | solution.py:168
  710.7 137.5 %all-reduce.11.cloned.1.call-done = (f32[64,16,32]{2,1,0:T(8,128)}, f32[1024,128]{1,0:T(8,128)}) async-done(((f32[64,16,32]{2,1,0:T(8,128)}, f32[1024,128]{1,0:T(8,128)}), (f32[64,16,32]{2,1,0:T(8,128)}, f32[1024,128]{1,0:T(8,128)})) %all-reduce.11.cloned.1.call-update) | async-done | bytes 655376 | tf_op jit(solution)/shard_map/psum | solution.py:17
  850.0 1.9 broadcast_multiply_fusion
  853.2 120.8 %all-reduce = (f32[64,32]{0,1:T(8,128)S(1)}, f32[64,32]{0,1:T(8,128)S(1)}) all-reduce(f32[64,32]{0,1:T(8,128)S(1)} %convolution_bitcast_fusion.1, f32[64,32]{0,1:T(8,128)S(1)} %convolution_bitcast_fusion), channel_id=1, replica_groups=mesh['row'=32,'col'=16] {'row'}, use_global_device_ids=true, to_apply=%region_11.12 | all-reduce | flops 4096 | bytes 32768 | tf_op jit(solution)/shard_map/psum | solution.py:11
  973.9 77.0 %all-reduce.2 = (f32[64,32]{0,1:T(8,128)S(1)}, f32[64,32]{0,1:T(8,128)S(1)}) all-reduce(f32[64,32]{0,1:T(8,128)S(1)} %get-tuple-element.4, f32[64,32]{0,1:T(8,128)S(1)} %get-tuple-element.5), channel_id=1, replica_groups=mesh['row'=32,'col'=16] {'col'}, use_global_device_ids=true, to_apply=%region_12.13 | all-reduce | flops 4096 | bytes 32768 | tf_op jit(solution)/shard_map/psum | solution.py:12
  (98 shorter events, 25.1 us)
Async XLA Ops:
  7.2 8.4 copy-start
  7.2 4.5 copy-start.1
  7.2 7.1 copy-start.16
  7.2 291.3 %all-reduce.13.cloned.1.call-start = ((), (), s32[]{:S(2)}) async-start(), calls=%async_computation.4 | async-start | bytes 1048576 | tf_op jit(solution)/shard_map/psum | solution.py:17
  7.3 8.2 copy-start.15
  9.2 613.8 %all-reduce.9.cloned.1.call-start = ((), (), s32[]{:S(2)}) async-start(), calls=%async_computation.2 | async-start | bytes 3145728 | tf_op jit(solution)/shard_map/psum | solution.py:172
  11.7 1.9 copy-start.14
  15.5 8.0 copy-start.11
  15.5 4.1 copy-start.9
  15.5 7.6 copy-start.7
  19.6 4.8 copy-start.13
  24.5 7.3 copy-start.5
  28.3 3.6 copy-start.4
  32.3 270.6 %copy-start.18 = (f32[64]{0:T(128)S(1)}, f32[64]{0:T(128)}, u32[]{:S(2)}) copy-start(f32[64]{0:T(128)} %param.8) | copy-start | bytes 772
  32.3 270.6 %copy-start.20 = (f32[64]{0:T(128)S(1)}, f32[64]{0:T(128)}, u32[]{:S(2)}) copy-start(f32[64]{0:T(128)} %param.9) | copy-start | bytes 772
  299.9 3.7 copy-start.17
  302.8 1.8 copy-start.12
  302.9 2.8 copy-start.6
  311.8 3.6 copy-start.10
  321.5 3.6 copy-start.2
  321.5 3.6 copy-start.8
  326.3 382.5 %reduce-scatter.2.cloned.1.call-start = ((), (), s32[]{:S(2)}) async-start(), calls=%async_computation.1 | async-start | bytes 557056 | tf_op jit(solution)/shard_map/reduce_scatter | solution.py:168
  328.2 523.7 %copy-start.19 = (f32[64]{0:T(128)S(1)}, f32[64]{0:T(128)}, u32[]{:S(2)}) copy-start(f32[64]{0:T(128)} %param.8) | copy-start | bytes 772
  328.3 520.0 %all-reduce.11.cloned.1.call-start = ((), (), s32[]{:S(2)}) async-start(), calls=%async_computation.3 | async-start | bytes 2097152 | tf_op jit(solution)/shard_map/psum | solution.py:17
  (1 other events, 0.7 us)
Sparse Core Ops, SparseCore 0:
  11.5 286.9 all-reduce.12
  326.5 296.4 all-reduce.8
  626.3 82.4 reduce-scatter.1
  711.6 136.6 all-reduce.10
